TPU v7x, 256 devices: a whole 4x4x8 slice. The times are simulated.
256 devices in a mesh: section: 8 (over z_hi, core), tp: 32 (over z_lo, x, y).
Axes of the slice: x: 4, y: 4, z: 8 (z_hi: 4, z_lo: 2; z = z_hi * 2 + z_lo), core: 2. Of those that a mesh axis runs over, the one named last changes fastest.
Arguments:
- start_tokens: bfloat16 [2, 32, 8192], P(None, None, 'tp'), may hold values from -6 to 6
- target_weight: bfloat16 [8, 8192, 8192], P('section', None, 'tp'), may hold values from -0.0625 to 0.0625
- online_weight: bfloat16 [8, 8192, 8192], P('section', 'tp'), may hold values from -0.0625 to 0.0625
- head_weight: bfloat16 [8192, 256], P('tp'), may hold values from -0.0625 to 0.0625
- reward: float32 [2, 32], P(None, 'section'), may hold values from -6 to 6
- action_bin: int32 [2, 32], P(None, 'section'), may hold values from 0 to 255
Outputs:
- target_value: float32 [2, 32], P(None, 'section')
- q_taken: float32 [2, 32], P(None, 'section')
All inputs are finite; a program needn't handle non-finite values.
Results may differ from a plain program's by a relative error of at most 0.018.
Values may be sent and summed in bfloat16 or wider, within the bound.
A program may use at most 64 MiB of HBM per device.

v0:
```python
import jax
import jax.numpy as jnp
from jax import lax
from jax.sharding import PartitionSpec as P


def shifted(block, axis, distance):
    devices = range(lax.axis_size(axis))
    route = [(i - distance, i) for i in devices if i - distance in devices]
    return lax.ppermute(block, axis, route)


def from_root(value, axis, source):
    kept = jnp.where(lax.axis_index(axis) == source, value, 0).astype(value.dtype)
    return lax.psum(kept, axis)


def per_device(start_tokens, target_weight, online_weight, head_weight, reward, action_bin):
    moved = lax.all_to_all(online_weight, "tp", split_axis=2, concat_axis=1, tiled=True)
    blended = (0.25 * moved.astype(jnp.float32) + 0.75 * target_weight.astype(jnp.float32)).astype(
        jnp.bfloat16
    )[0]
    sections = lax.axis_size("section")
    position = lax.axis_index("section")
    micro = start_tokens.shape[0]
    finished = jnp.zeros(start_tokens.shape, jnp.bfloat16)
    incoming = jnp.zeros(start_tokens.shape[1:], jnp.bfloat16)

    def advance(tick, carry):
        incoming, finished = carry
        fresh = lax.dynamic_index_in_dim(
            start_tokens, jnp.minimum(tick, micro - 1), 0, keepdims=False
        )
        source = jnp.where(position == 0, fresh, incoming)
        local = source.astype(jnp.float32)
        whole = lax.all_gather(source, "tp", axis=1, tiled=True)
        wide = whole.astype(jnp.float32)
        normed = (wide * lax.rsqrt(jnp.mean(wide * wide, axis=1, keepdims=True) + 1e-06)).astype(
            jnp.bfloat16
        )
        result = (local + jnp.dot(normed, blended, preferred_element_type=jnp.float32)).astype(
            jnp.bfloat16
        )
        slot = tick - (sections - 1)
        keep = jnp.logical_and(position == sections - 1, slot >= 0)
        placed = lax.dynamic_update_index_in_dim(finished, result, jnp.clip(slot, 0, micro - 1), 0)
        finished = jnp.where(keep, placed, finished)
        incoming = shifted(result, "section", 1)
        return (incoming, finished)

    incoming, finished = lax.fori_loop(0, micro + sections - 1, advance, (incoming, finished))
    outputs = from_root(finished, "section", sections - 1)
    share_rows = reward.shape[1]
    mine = lax.dynamic_slice_in_dim(outputs, position * share_rows, share_rows, 1)
    mine = mine.reshape(micro * share_rows, mine.shape[2])
    partial_value = jnp.dot(mine, head_weight, preferred_element_type=jnp.float32)
    actions = action_bin.reshape(micro * share_rows, 1)
    values = lax.psum(partial_value, "tp")
    best = jnp.max(values, axis=1)
    chosen = (jnp.arange(values.shape[1], dtype=jnp.int32)[None, :] == actions).astype(jnp.float32)
    taken = jnp.sum(values * chosen, axis=1)
    best = best.reshape(micro, share_rows)
    taken = taken.reshape(micro, share_rows)
    return (reward + 0.98 * best, taken)


def solution(mesh):
    in_specs = (
        P(None, None, "tp"),
        P("section", None, "tp"),
        P("section", "tp", None),
        P("tp", None),
        P(None, "section"),
        P(None, "section"),
    )
    out_specs = (P(None, "section"), P(None, "section"))
    return jax.shard_map(
        per_device, mesh=mesh, in_specs=in_specs, out_specs=out_specs, check_vma=False
    )
```

profile of v0, /device:TPU:1, one launch (start us, length us, event | category | flops | bytes accessed | tf_op | source)
XLA Modules:
  0.0 1090.9 jit_solution(2322913025078302848)
XLA Ops:
  19.0 43.5 %reduce = bf16[8192,256]{1,0:T(8,128)(2,1)} reduce(bf16[8192,1,256]{2,1,0:T(2,128)(2,1)} %bitcast.27, bf16[]{:T(256)} %broadcast.66), dimensions={1}, to_apply=%bitcast.14.reduce_sub_computation | reduce | bytes 8388610
  78.9 49.5 %all-to-all-done = bf16[32,2,32768]{2,1,0:T(2,128)(2,1)} async-done(((bf16[32,2,32768]{2,1,0:T(2,128)(2,1)}), bf16[32,2,32768]{2,1,0:T(2,128)(2,1)}, u32[]{:S(2)}, u32[]{:S(2)}) %all-to-all-start) | async-done | bytes 4194336 | tf_op jit(solution)/shard_map/all_to_all | solution.py:19
  128.4 19.8 %reshape.51 = bf16[8192,1,256]{2,1,0:T(2,128)(2,1)} reshape(bf16[32,2,32768]{2,1,0:T(2,128)(2,1)} %all-to-all-done) | data formatting | bytes 8388608
  159.0 19.2 %copy.10 = f32[1,32,256,256]{3,2,1,0:T(8,128)} copy(f32[1,32,256,256]{2,0,3,1:T(1,128)} %bitcast.28) | data formatting | bytes 16777216 | tf_op jit(solution)/shard_map/mul | solution.py:20
  185.8 803.3 %while.17 = (s32[]{:T(128)}, bf16[32,256]{1,0:T(8,128)(2,1)S(1)}, bf16[2,32,256]{2,1,0:T(8,128)(2,1)S(1)}, pred[]{:T(512)}, bf16[2,32,256]{2,1,0:T(8,128)(2,1)S(...) while((s32[]{:T(128)}, bf16[32,256]{1,0:T(8,128)(2,1)S(1)}, ...), condition=%wide.region_2.3_spmd, body=%wide.region_0.2_spmd.sunk | while | flops 135831600 | bytes 5964925 | solution.py:51
  185.8 73.1 %all_gather.11 = bf16[32,8192]{1,0:T(8,128)(2,1)S(1)} all-gather(bf16[32,256]{1,0:T(8,128)(2,1)S(1)} %bitcast_select_fusion.3), channel_id=1, replica_groups=mesh['section'=8,'tp'=32] {'tp'}, dimensions={1}, use_global_device_ids=true | all-gather | bytes 540672 | tf_op jit(solution)/shard_map/while/body/eval_jaxpr/all_gather | solution.py:36
  262.2 19.3 %collective-permute-start = (bf16[32,256]{1,0:T(8,128)(2,1)S(1)}, bf16[32,256]{1,0:T(8,128)(2,1)S(1)}, u32[]{:S(2)}, u32[]{:S(2)}) collective-permute-start(bf16[32,256]{1,0:T(8,128)(2,1)S(1)} %get-tuple-element.227), channel_id=1, source_target_pairs={{0,32},{32,64},{64,96},{96,128},{128,160},{160,192},{192,224},{1,3... | collective-permute-start | bytes 49160 | tf_op jit(solution)/shard_map/while/body/eval_jaxpr/ppermute | solution.py:10
  282.4 64.5 %all_gather.11 = bf16[32,8192]{1,0:T(8,128)(2,1)S(1)} all-gather(bf16[32,256]{1,0:T(8,128)(2,1)S(1)} %bitcast_select_fusion.3), channel_id=1, replica_groups=mesh['section'=8,'tp'=32] {'tp'}, dimensions={1}, use_global_device_ids=true | all-gather | bytes 540672 | tf_op jit(solution)/shard_map/while/body/eval_jaxpr/all_gather | solution.py:36
  350.2 18.7 %collective-permute-start = (bf16[32,256]{1,0:T(8,128)(2,1)S(1)}, bf16[32,256]{1,0:T(8,128)(2,1)S(1)}, u32[]{:S(2)}, u32[]{:S(2)}) collective-permute-start(bf16[32,256]{1,0:T(8,128)(2,1)S(1)} %get-tuple-element.227), channel_id=1, source_target_pairs={{0,32},{32,64},{64,96},{96,128},{128,160},{160,192},{192,224},{1,3... | collective-permute-start | bytes 49160 | tf_op jit(solution)/shard_map/while/body/eval_jaxpr/ppermute | solution.py:10
  369.8 66.1 %all_gather.11 = bf16[32,8192]{1,0:T(8,128)(2,1)S(1)} all-gather(bf16[32,256]{1,0:T(8,128)(2,1)S(1)} %bitcast_select_fusion.3), channel_id=1, replica_groups=mesh['section'=8,'tp'=32] {'tp'}, dimensions={1}, use_global_device_ids=true | all-gather | bytes 540672 | tf_op jit(solution)/shard_map/while/body/eval_jaxpr/all_gather | solution.py:36
  439.2 19.0 %collective-permute-start = (bf16[32,256]{1,0:T(8,128)(2,1)S(1)}, bf16[32,256]{1,0:T(8,128)(2,1)S(1)}, u32[]{:S(2)}, u32[]{:S(2)}) collective-permute-start(bf16[32,256]{1,0:T(8,128)(2,1)S(1)} %get-tuple-element.227), channel_id=1, source_target_pairs={{0,32},{32,64},{64,96},{96,128},{128,160},{160,192},{192,224},{1,3... | collective-permute-start | bytes 49160 | tf_op jit(solution)/shard_map/while/body/eval_jaxpr/ppermute | solution.py:10
  459.1 64.1 %all_gather.11 = bf16[32,8192]{1,0:T(8,128)(2,1)S(1)} all-gather(bf16[32,256]{1,0:T(8,128)(2,1)S(1)} %bitcast_select_fusion.3), channel_id=1, replica_groups=mesh['section'=8,'tp'=32] {'tp'}, dimensions={1}, use_global_device_ids=true | all-gather | bytes 540672 | tf_op jit(solution)/shard_map/while/body/eval_jaxpr/all_gather | solution.py:36
  526.5 19.1 %collective-permute-start = (bf16[32,256]{1,0:T(8,128)(2,1)S(1)}, bf16[32,256]{1,0:T(8,128)(2,1)S(1)}, u32[]{:S(2)}, u32[]{:S(2)}) collective-permute-start(bf16[32,256]{1,0:T(8,128)(2,1)S(1)} %get-tuple-element.227), channel_id=1, source_target_pairs={{0,32},{32,64},{64,96},{96,128},{128,160},{160,192},{192,224},{1,3... | collective-permute-start | bytes 49160 | tf_op jit(solution)/shard_map/while/body/eval_jaxpr/ppermute | solution.py:10
  546.5 65.7 %all_gather.11 = bf16[32,8192]{1,0:T(8,128)(2,1)S(1)} all-gather(bf16[32,256]{1,0:T(8,128)(2,1)S(1)} %bitcast_select_fusion.3), channel_id=1, replica_groups=mesh['section'=8,'tp'=32] {'tp'}, dimensions={1}, use_global_device_ids=true | all-gather | bytes 540672 | tf_op jit(solution)/shard_map/while/body/eval_jaxpr/all_gather | solution.py:36
  615.5 19.4 %collective-permute-start = (bf16[32,256]{1,0:T(8,128)(2,1)S(1)}, bf16[32,256]{1,0:T(8,128)(2,1)S(1)}, u32[]{:S(2)}, u32[]{:S(2)}) collective-permute-start(bf16[32,256]{1,0:T(8,128)(2,1)S(1)} %get-tuple-element.227), channel_id=1, source_target_pairs={{0,32},{32,64},{64,96},{96,128},{128,160},{160,192},{192,224},{1,3... | collective-permute-start | bytes 49160 | tf_op jit(solution)/shard_map/while/body/eval_jaxpr/ppermute | solution.py:10
  635.8 64.5 %all_gather.11 = bf16[32,8192]{1,0:T(8,128)(2,1)S(1)} all-gather(bf16[32,256]{1,0:T(8,128)(2,1)S(1)} %bitcast_select_fusion.3), channel_id=1, replica_groups=mesh['section'=8,'tp'=32] {'tp'}, dimensions={1}, use_global_device_ids=true | all-gather | bytes 540672 | tf_op jit(solution)/shard_map/while/body/eval_jaxpr/all_gather | solution.py:36
  703.6 18.9 %collective-permute-start = (bf16[32,256]{1,0:T(8,128)(2,1)S(1)}, bf16[32,256]{1,0:T(8,128)(2,1)S(1)}, u32[]{:S(2)}, u32[]{:S(2)}) collective-permute-start(bf16[32,256]{1,0:T(8,128)(2,1)S(1)} %get-tuple-element.227), channel_id=1, source_target_pairs={{0,32},{32,64},{64,96},{96,128},{128,160},{160,192},{192,224},{1,3... | collective-permute-start | bytes 49160 | tf_op jit(solution)/shard_map/while/body/eval_jaxpr/ppermute | solution.py:10
  723.3 65.7 %all_gather.11 = bf16[32,8192]{1,0:T(8,128)(2,1)S(1)} all-gather(bf16[32,256]{1,0:T(8,128)(2,1)S(1)} %bitcast_select_fusion.3), channel_id=1, replica_groups=mesh['section'=8,'tp'=32] {'tp'}, dimensions={1}, use_global_device_ids=true | all-gather | bytes 540672 | tf_op jit(solution)/shard_map/while/body/eval_jaxpr/all_gather | solution.py:36
  792.4 19.2 %collective-permute-start = (bf16[32,256]{1,0:T(8,128)(2,1)S(1)}, bf16[32,256]{1,0:T(8,128)(2,1)S(1)}, u32[]{:S(2)}, u32[]{:S(2)}) collective-permute-start(bf16[32,256]{1,0:T(8,128)(2,1)S(1)} %get-tuple-element.227), channel_id=1, source_target_pairs={{0,32},{32,64},{64,96},{96,128},{128,160},{160,192},{192,224},{1,3... | collective-permute-start | bytes 49160 | tf_op jit(solution)/shard_map/while/body/eval_jaxpr/ppermute | solution.py:10
  812.5 64.5 %all_gather.11 = bf16[32,8192]{1,0:T(8,128)(2,1)S(1)} all-gather(bf16[32,256]{1,0:T(8,128)(2,1)S(1)} %bitcast_select_fusion.3), channel_id=1, replica_groups=mesh['section'=8,'tp'=32] {'tp'}, dimensions={1}, use_global_device_ids=true | all-gather | bytes 540672 | tf_op jit(solution)/shard_map/while/body/eval_jaxpr/all_gather | solution.py:36
  880.3 18.9 %collective-permute-start = (bf16[32,256]{1,0:T(8,128)(2,1)S(1)}, bf16[32,256]{1,0:T(8,128)(2,1)S(1)}, u32[]{:S(2)}, u32[]{:S(2)}) collective-permute-start(bf16[32,256]{1,0:T(8,128)(2,1)S(1)} %get-tuple-element.227), channel_id=1, source_target_pairs={{0,32},{32,64},{64,96},{96,128},{128,160},{160,192},{192,224},{1,3... | collective-permute-start | bytes 49160 | tf_op jit(solution)/shard_map/while/body/eval_jaxpr/ppermute | solution.py:10
  900.0 66.6 %all_gather.11 = bf16[32,8192]{1,0:T(8,128)(2,1)S(1)} all-gather(bf16[32,256]{1,0:T(8,128)(2,1)S(1)} %bitcast_select_fusion.3), channel_id=1, replica_groups=mesh['section'=8,'tp'=32] {'tp'}, dimensions={1}, use_global_device_ids=true | all-gather | bytes 540672 | tf_op jit(solution)/shard_map/while/body/eval_jaxpr/all_gather | solution.py:36
  989.1 36.2 %psum.14 = bf16[2,32,256]{2,1,0:T(8,128)(2,1)S(1)} all-reduce(bf16[2,32,256]{2,1,0:T(8,128)(2,1)S(1)} %broadcast_select_fusion), channel_id=1, replica_groups=mesh['section'=8,'tp'=32] {'section'}, use_global_device_ids=true, to_apply=%region_3.4 | all-reduce | flops 16384 | bytes 65536 | tf_op jit(solution)/shard_map/psum | solution.py:15
  1025.5 63.9 %psum.15 = f32[8,256]{1,0:T(8,128)S(1)} all-reduce(f32[8,256]{1,0:T(8,128)S(1)} %fusion.7), channel_id=1, replica_groups=mesh['section'=8,'tp'=32] {'tp'}, use_global_device_ids=true, to_apply=%region_4.5 | all-reduce | flops 2048 | bytes 16384 | tf_op jit(solution)/shard_map/psum | solution.py:58
  (72 shorter events, 110.6 us)
Async XLA Ops:
  0.6 1024.7 %copy-start = (bf16[256,256]{1,0:T(8,128)(2,1)S(1)}, bf16[256,256]{1,0:T(8,128)(2,1)}, u32[]{:S(2)}) copy-start(bf16[256,256]{1,0:T(8,128)(2,1)} %param.11) | copy-start | bytes 393220
  62.5 16.3 %copy-start.3 = (s32[2,4]{1,0:T(2,128)S(1)}, s32[2,4]{1,0:T(2,128)}, u32[]{:S(2)}) copy-start(s32[2,4]{1,0:T(2,128)} %param.13) | copy-start | bytes 100
  69.5 59.0 %all-to-all-start = ((bf16[32,2,32768]{2,1,0:T(2,128)(2,1)}), bf16[32,2,32768]{2,1,0:T(2,128)(2,1)}, u32[]{:S(2)}, u32[]{:S(2)}) async-start(bf16[32,2,32768]{2,1,0:T(2,128)(2,1)} %reshape.50), calls=%async_computation | async-start | bytes 8388608 | tf_op jit(solution)/shard_map/all_to_all | solution.py:19
  178.2 7.5 copy-start.1
  185.8 904.5 %copy-start.2 = (f32[2,4]{1,0:T(2,128)S(1)}, f32[2,4]{1,0:T(2,128)}, u32[]{:S(2)}) copy-start(f32[2,4]{1,0:T(2,128)} %param.12) | copy-start | bytes 100
  262.2 20.1 %collective-permute-start = (bf16[32,256]{1,0:T(8,128)(2,1)S(1)}, bf16[32,256]{1,0:T(8,128)(2,1)S(1)}, u32[]{:S(2)}, u32[]{:S(2)}) collective-permute-start(bf16[32,256]{1,0:T(8,128)(2,1)S(1)} %get-tuple-element.227), channel_id=1, source_target_pairs={{0,32},{32,64},{64,96},{96,128},{128,160},{160,192},{192,224},{1,3... | collective-permute-start | bytes 49160 | tf_op jit(solution)/shard_map/while/body/eval_jaxpr/ppermute | solution.py:10
  350.2 19.5 %collective-permute-start = (bf16[32,256]{1,0:T(8,128)(2,1)S(1)}, bf16[32,256]{1,0:T(8,128)(2,1)S(1)}, u32[]{:S(2)}, u32[]{:S(2)}) collective-permute-start(bf16[32,256]{1,0:T(8,128)(2,1)S(1)} %get-tuple-element.227), channel_id=1, source_target_pairs={{0,32},{32,64},{64,96},{96,128},{128,160},{160,192},{192,224},{1,3... | collective-permute-start | bytes 49160 | tf_op jit(solution)/shard_map/while/body/eval_jaxpr/ppermute | solution.py:10
  439.2 19.9 %collective-permute-start = (bf16[32,256]{1,0:T(8,128)(2,1)S(1)}, bf16[32,256]{1,0:T(8,128)(2,1)S(1)}, u32[]{:S(2)}, u32[]{:S(2)}) collective-permute-start(bf16[32,256]{1,0:T(8,128)(2,1)S(1)} %get-tuple-element.227), channel_id=1, source_target_pairs={{0,32},{32,64},{64,96},{96,128},{128,160},{160,192},{192,224},{1,3... | collective-permute-start | bytes 49160 | tf_op jit(solution)/shard_map/while/body/eval_jaxpr/ppermute | solution.py:10
  526.5 20.0 %collective-permute-start = (bf16[32,256]{1,0:T(8,128)(2,1)S(1)}, bf16[32,256]{1,0:T(8,128)(2,1)S(1)}, u32[]{:S(2)}, u32[]{:S(2)}) collective-permute-start(bf16[32,256]{1,0:T(8,128)(2,1)S(1)} %get-tuple-element.227), channel_id=1, source_target_pairs={{0,32},{32,64},{64,96},{96,128},{128,160},{160,192},{192,224},{1,3... | collective-permute-start | bytes 49160 | tf_op jit(solution)/shard_map/while/body/eval_jaxpr/ppermute | solution.py:10
  615.5 20.2 %collective-permute-start = (bf16[32,256]{1,0:T(8,128)(2,1)S(1)}, bf16[32,256]{1,0:T(8,128)(2,1)S(1)}, u32[]{:S(2)}, u32[]{:S(2)}) collective-permute-start(bf16[32,256]{1,0:T(8,128)(2,1)S(1)} %get-tuple-element.227), channel_id=1, source_target_pairs={{0,32},{32,64},{64,96},{96,128},{128,160},{160,192},{192,224},{1,3... | collective-permute-start | bytes 49160 | tf_op jit(solution)/shard_map/while/body/eval_jaxpr/ppermute | solution.py:10
  703.6 19.7 %collective-permute-start = (bf16[32,256]{1,0:T(8,128)(2,1)S(1)}, bf16[32,256]{1,0:T(8,128)(2,1)S(1)}, u32[]{:S(2)}, u32[]{:S(2)}) collective-permute-start(bf16[32,256]{1,0:T(8,128)(2,1)S(1)} %get-tuple-element.227), channel_id=1, source_target_pairs={{0,32},{32,64},{64,96},{96,128},{128,160},{160,192},{192,224},{1,3... | collective-permute-start | bytes 49160 | tf_op jit(solution)/shard_map/while/body/eval_jaxpr/ppermute | solution.py:10
  792.4 20.1 %collective-permute-start = (bf16[32,256]{1,0:T(8,128)(2,1)S(1)}, bf16[32,256]{1,0:T(8,128)(2,1)S(1)}, u32[]{:S(2)}, u32[]{:S(2)}) collective-permute-start(bf16[32,256]{1,0:T(8,128)(2,1)S(1)} %get-tuple-element.227), channel_id=1, source_target_pairs={{0,32},{32,64},{64,96},{96,128},{128,160},{160,192},{192,224},{1,3... | collective-permute-start | bytes 49160 | tf_op jit(solution)/shard_map/while/body/eval_jaxpr/ppermute | solution.py:10
  880.3 19.7 %collective-permute-start = (bf16[32,256]{1,0:T(8,128)(2,1)S(1)}, bf16[32,256]{1,0:T(8,128)(2,1)S(1)}, u32[]{:S(2)}, u32[]{:S(2)}) collective-permute-start(bf16[32,256]{1,0:T(8,128)(2,1)S(1)} %get-tuple-element.227), channel_id=1, source_target_pairs={{0,32},{32,64},{64,96},{96,128},{128,160},{160,192},{192,224},{1,3... | collective-permute-start | bytes 49160 | tf_op jit(solution)/shard_map/while/body/eval_jaxpr/ppermute | solution.py:10
  969.9 19.2 %collective-permute-start = (bf16[32,256]{1,0:T(8,128)(2,1)S(1)}, bf16[32,256]{1,0:T(8,128)(2,1)S(1)}, u32[]{:S(2)}, u32[]{:S(2)}) collective-permute-start(bf16[32,256]{1,0:T(8,128)(2,1)S(1)} %get-tuple-element.227), channel_id=1, source_target_pairs={{0,32},{32,64},{64,96},{96,128},{128,160},{160,192},{192,224},{1,3... | collective-permute-start | bytes 49160 | tf_op jit(solution)/shard_map/while/body/eval_jaxpr/ppermute | solution.py:10
where the time goes:
time: 1110 us; the launch traced here: 1090 us
  blocking collectives  695 us (63%)
  starting transfers between devices  180 us (16%)
  local copies, waits for them, and re-layouts  65.1 us (6%)
  other arithmetic  64.9 us (6%)
  waiting for transfers between devices  57.1 us (5%)
  matrix products  27.7 us (2%)
    all_gather x9, blocking collectives, advance(): whole = lax.all_gather(source, 'tp', axis=1, tiled=True)  595 us
    ppermute x9, starting transfers between devices, shifted(): return lax.ppermute(block, axis, route)  171 us
    psum x1, blocking collectives, per_device(): values = lax.psum(partial_value, 'tp')  63.9 us
    all_to_all x1, waiting for transfers between devices, per_device(): lax.all_to_all(online_weight, 'tp', split_axis=2, concat_axis=1, tiled=True)  49.5 us
    unnamed x12, local copies, waits for them, and re-layouts  45.1 us
    unnamed x1, other arithmetic  43.5 us
    psum x1, blocking collectives, from_root(): return lax.psum(kept, axis)  36.2 us
    dot_general x9, matrix products, advance(): jnp.dot(normed, blended, preferred_element_type=jnp.float32)  27.6 us
  transfers between devices with their start and end apart: 10, of which 10 were waited for; matrix products, arithmetic and copies ran while one was open for 0% of the time, Pallas kernels for 0%

commit v1 on v0

v1 whole, which is shorter than its diff:
```python
import functools

import jax
import jax.numpy as jnp
from jax import lax
from jax.experimental import pallas as pl
from jax.experimental.pallas import tpu as pltpu
from jax.sharding import PartitionSpec as P

MESH = pl.DeviceIdType.MESH
SECTIONS = 8
PEERS = 32
ROWS = 64
WIDTH = 256
DEPTH = PEERS * WIDTH
CHUNKS = 4
AHEAD = 2
PART = ROWS // CHUNKS
OWNED = 8


def place(tp):
    return tp // 16, lax.rem(tp // 4, 4), lax.rem(tp, 4)


def index(z, x, y):
    return z * 16 + x * 4 + y


def far(v):
    return v + v // 2 - 2 * (v // 3)


def peer(tp, step):
    z, x, y = place(tp)
    return index(
        lax.rem(z + step // 16, 2),
        lax.rem(x + far(lax.rem(step // 4, 4)), 4),
        lax.rem(y + far(lax.rem(step, 4)), 4),
    )


def kernel(
    start_ref, target_ref, online_ref, head_ref, reward_ref, action_ref, value_ref, taken_ref,
    target, online, hidden, shares, sends, result, scores, gathered, summed, finals,
    load_sem, own_sem, all_sem, share_sem, all_out, next_out, share_out, score_sem, score_out, final_sem, final_out,
):
    section = lax.axis_index("section")
    me = lax.axis_index("tp")
    z, x, y = place(me)
    odd = lax.rem(section, 2)
    even = odd == 0
    last = section == SECTIONS - 1
    my_micro, bit = y // 2, lax.rem(y, 2)
    my_block = (1 - bit) * (1 - z) + bit * (2 + z)

    def owner(micro, block):
        return index(lax.rem((block + 1) // 2 + 1, 2), x, 2 * micro + block // 2)

    def remote(src, dst, out, sem, at_section, tp):
        return pltpu.make_async_remote_copy(
            src_ref=src, dst_ref=dst, send_sem=out, recv_sem=sem,
            device_id={"section": at_section, "tp": tp}, device_id_type=MESH,
        )

    def settle(ref, sem):
        pltpu.make_async_copy(ref, ref, sem).wait()

    load_online = pltpu.make_async_copy(online_ref, online, load_sem.at[0])
    load_target = pltpu.make_async_copy(target_ref, target, load_sem.at[1])
    load_online.start()
    load_target.start()

    @pl.when(section == 0)
    def _():
        for c in range(CHUNKS):
            pltpu.make_async_copy(
                start_ref.at[pl.ds(c * PART, PART)], hidden.at[c, me], own_sem.at[c]
            ).start()

    barrier = pltpu.get_barrier_semaphore()

    def greet(at_section, tp):
        pl.semaphore_signal(
            barrier, inc=1, device_id={"section": at_section, "tp": tp}, device_id_type=MESH
        )

    @pl.loop(1, PEERS)
    def _(i):
        greet(section, peer(me, PEERS - i))

    @pl.when(odd == 1)
    def _():
        @pl.loop(0, PEERS)
        def _(i):
            greet(section - 1, peer(me, PEERS - 1 - i))

    @pl.when(jnp.logical_and(even, section > 0))
    def _():
        greet(section - 1, me)

    for micro in range(2):
        mine = owner(micro, section // 2)

        @pl.when(jnp.logical_not(jnp.logical_and(last, mine == me)))
        def _():
            greet(SECTIONS - 1, mine)

    @pl.when(even)
    def _():
        pl.semaphore_wait(barrier, 2 * PEERS - 1)

    @pl.when(jnp.logical_and(odd == 1, section < SECTIONS - 1))
    def _():
        pl.semaphore_wait(barrier, PEERS)

    @pl.when(jnp.logical_and(last, my_block != 3))
    def _():
        pl.semaphore_wait(barrier, PEERS - 1 + 16)

    @pl.when(jnp.logical_and(last, my_block == 3))
    def _():
        pl.semaphore_wait(barrier, PEERS - 1 + 15)

    load_online.wait()
    load_target.wait()

    def send(c):
        settle(hidden.at[c, 0], own_sem.at[c])

        @pl.when(even)
        def _():
            @pl.loop(1, PEERS)
            def _(i):
                remote(
                    hidden.at[c, me], hidden.at[c, me], all_out.at[c], all_sem.at[c], section, peer(me, PEERS - i)
                ).start()

        own = hidden[c, me]
        for group in range(4):
            steps = [PEERS - 1 - 8 * group - u for u in range(8)]
            for step in steps:
                tp = peer(me, step)
                part = jnp.dot(
                    own,
                    online[:, pl.ds(pl.multiple_of(tp * WIDTH, WIDTH), WIDTH)],
                    preferred_element_type=jnp.float32,
                ).astype(jnp.bfloat16)
                if step == 0:
                    shares[c, me] = part
                else:
                    sends[c, tp] = part
            for step in steps:
                if step > 0:
                    tp = peer(me, step)
                    remote(
                        sends.at[c, tp], shares.at[c, me], share_out.at[c], share_sem.at[c], section, tp
                    ).start()

    def reduce(c):
        settle(hidden.at[c, pl.ds(0, PEERS - 1)], all_sem.at[c])
        product = jnp.zeros((PART, WIDTH), jnp.float32)
        square = jnp.zeros((PART, WIDTH), jnp.float32)
        for tp in range(PEERS):
            block = hidden[c, tp]
            product += jnp.dot(
                block, target[pl.ds(tp * WIDTH, WIDTH), :], preferred_element_type=jnp.float32
            )
            wide = block.astype(jnp.float32)
            square += wide * wide
        scale = lax.rsqrt(jnp.sum(square, axis=1, keepdims=True) * (1.0 / DEPTH) + 1e-06)
        settle(shares.at[c, pl.ds(0, PEERS - 1)], share_sem.at[c])
        total = jnp.zeros((PART, WIDTH), jnp.float32)
        for tp in range(PEERS):
            total += shares[c, tp].astype(jnp.float32)
        out = (
            hidden[c, me].astype(jnp.float32) + scale * (0.75 * product + 0.25 * total)
        ).astype(jnp.bfloat16)
        result[c] = out

        @pl.when(even)
        def _():
            @pl.loop(0, PEERS - 1)
            def _(i):
                remote(
                    result.at[c], hidden.at[c, me], next_out.at[c], all_sem.at[c], section + 1, peer(me, PEERS - 1 - i)
                ).start()

        @pl.when(section < SECTIONS - 1)
        def _():
            remote(
                result.at[c], hidden.at[c, me], next_out.at[c], own_sem.at[c], section + 1, me
            ).start()

        @pl.when(last)
        def _():
            partial = jnp.dot(out, head_ref[...], preferred_element_type=jnp.float32)
            for half in range(PART // OWNED):
                group = c * (PART // OWNED) + half
                rows = partial[half * OWNED : (half + 1) * OWNED]
                scores[group] = rows
                first = owner(group // 4, lax.rem(group, 4))
                for column in range(4):
                    tp = first + (column - x) * 4

                    @pl.when(tp == me)
                    def _():
                        gathered[me] = rows

                    @pl.when(tp != me)
                    def _():
                        remote(
                            scores.at[group], gathered.at[me], score_out, score_sem, section, tp
                        ).start()

    @pl.loop(0, CHUNKS + AHEAD)
    def _(step):
        @pl.when(step < CHUNKS)
        def _():
            send(step)

        @pl.when(step >= AHEAD)
        def _():
            reduce(step - AHEAD)

    @pl.when(last)
    def _():
        settle(gathered.at[pl.ds(0, PEERS - 1)], score_sem)
        total = jnp.zeros((OWNED, WIDTH), jnp.float32)
        for tp in range(PEERS):
            total += gathered[tp]
        summed[...] = total
        for i in range(16):
            at_section = 2 * my_block + i // 8
            tp = index((i // 4) % 2, x, i % 4)
            local = jnp.logical_and(at_section == section, tp == me)

            @pl.when(local)
            def _():
                pltpu.make_async_copy(summed, finals.at[my_micro], final_sem.at[my_micro]).start()

            @pl.when(jnp.logical_not(local))
            def _():
                remote(
                    summed, finals.at[my_micro], final_out, final_sem.at[my_micro], at_section, tp
                ).start()

    lane = lax.broadcasted_iota(jnp.int32, (OWNED, WIDTH), 1)
    row = lax.broadcasted_iota(jnp.int32, (OWNED, WIDTH), 0) - 4 * odd
    for micro in range(2):
        settle(finals.at[micro], final_sem.at[micro])
        q = finals[micro]
        action = jnp.zeros((OWNED, WIDTH), jnp.int32)
        for token in range(4):
            action = jnp.where(row == token, action_ref[micro, token], action)
        best = jnp.max(q, axis=1, keepdims=True)
        taken = jnp.sum(jnp.where(lane == action, q, 0.0), axis=1, keepdims=True)
        best = jnp.sum(jnp.where(lane == row, best, 0.0), axis=0, keepdims=True)
        taken = jnp.sum(jnp.where(lane == row, taken, 0.0), axis=0, keepdims=True)
        value_ref[pl.ds(micro, 1), :] = reward_ref[pl.ds(micro, 1), :] + 0.98 * best[:, :4]
        taken_ref[pl.ds(micro, 1), :] = taken[:, :4]

    most = PEERS - 1

    @pl.loop(0, CHUNKS)
    def _(c):
        settle(sends.at[c, pl.ds(0, most)], share_out.at[c])

        @pl.when(even)
        def _():
            settle(hidden.at[c, pl.ds(0, most)], all_out.at[c])
            settle(hidden.at[c], next_out.at[c])

        @pl.when(jnp.logical_and(odd == 1, section < SECTIONS - 1))
        def _():
            settle(hidden.at[c, 0], next_out.at[c])

    @pl.when(last)
    def _():
        settle(gathered.at[pl.ds(0, most)], score_out)

        @pl.when(my_block != 3)
        def _():
            settle(gathered.at[pl.ds(0, 16)], final_out)

        @pl.when(my_block == 3)
        def _():
            settle(gathered.at[pl.ds(0, 15)], final_out)


def per_device(start_tokens, target_weight, online_weight, head_weight, reward, action_bin):
    bf16, f32 = jnp.bfloat16, jnp.float32
    dma = pltpu.SemaphoreType.DMA
    shape = jax.ShapeDtypeStruct(reward.shape, f32)
    anywhere = pl.BlockSpec(memory_space=pl.ANY)
    vmem = pl.BlockSpec(memory_space=pltpu.VMEM)
    blocks = pltpu.VMEM((CHUNKS, PEERS, PART, WIDTH), bf16)
    return pl.pallas_call(
        kernel,
        out_shape=(shape, shape),
        in_specs=[anywhere, anywhere, anywhere, vmem, vmem, pl.BlockSpec(memory_space=pltpu.SMEM)],
        out_specs=(vmem, vmem),
        scratch_shapes=[
            pltpu.VMEM((DEPTH, WIDTH), bf16),
            pltpu.VMEM((WIDTH, DEPTH), bf16),
            blocks,
            blocks,
            blocks,
            pltpu.VMEM((CHUNKS, PART, WIDTH), bf16),
            pltpu.VMEM((ROWS // OWNED, OWNED, WIDTH), f32),
            pltpu.VMEM((PEERS, OWNED, WIDTH), f32),
            pltpu.VMEM((OWNED, WIDTH), f32),
            pltpu.VMEM((2, OWNED, WIDTH), f32),
            dma((2,)),
            dma((CHUNKS,)),
            dma((CHUNKS,)),
            dma((CHUNKS,)),
            dma((CHUNKS,)),
            dma((CHUNKS,)),
            dma((CHUNKS,)),
            dma,
            dma,
            dma((2,)),
            dma,
        ],
        name="relay",
        compiler_params=pltpu.CompilerParams(collective_id=0, has_side_effects=True),
    )(
        start_tokens.reshape(ROWS, WIDTH),
        target_weight.reshape(DEPTH, WIDTH),
        online_weight.reshape(WIDTH, DEPTH),
        head_weight,
        reward,
        action_bin,
    )


def solution(mesh):
    in_specs = (
        P(None, None, "tp"),
        P("section", None, "tp"),
        P("section", "tp", None),
        P("tp", None),
        P(None, "section"),
        P(None, "section"),
    )
    out_specs = (P(None, "section"), P(None, "section"))
    return jax.shard_map(
        per_device, mesh=mesh, in_specs=in_specs, out_specs=out_specs, check_vma=False
    )
```

time: 1110 us -> 121 us (0.11); the launches traced: 1090 us -> 121 us
  blocking collectives: 695 us -> 0 us
  starting transfers between devices: 180 us -> 0 us
  Pallas kernels: 0 us -> 118 us
  other arithmetic: 64.9 us -> 0 us
  local copies, waits for them, and re-layouts: 65.1 us -> 2.44 us
  waiting for transfers between devices: 57.1 us -> 0 us
  matrix products: 27.7 us -> 0 us
    all_gather x9 -> x0, blocking collectives: 595 us -> none  [advance(): whole = lax.all_gather(source, 'tp', axis=1, tiled=True)]
    ppermute x9 -> x0, starting transfers between devices: 171 us -> none  [shifted(): return lax.ppermute(block, axis, route)]
    pallas_call x0 -> x1, Pallas kernels: none -> 118 us  [per_device(): pl.pallas_call(kernel, out_shape=(shape, shape), in_specs=[anywhere, anyw...]
    psum x2 -> x0, blocking collectives: 100 us -> none  [the longest x1 63.9 us: per_device(): values = lax.psum(partial_value, 'tp')]
    all_to_all x1 -> x0, waiting for transfers between devices: 49.5 us -> none  [per_device(): lax.all_to_all(online_weight, 'tp', split_axis=2, concat_axis=1, tiled=True)]
    unnamed x1 -> x0, other arithmetic: 43.5 us -> none
    unnamed x12 -> x2, local copies, waits for them, and re-layouts: 45.1 us -> 2.44 us
    dot_general x10 -> x0, matrix products: 27.7 us -> none  [the longest x9 27.6 us: advance(): jnp.dot(normed, blended, preferred_element_type=jnp.float32)]
  transfers between devices with their start and end apart: 10 -> 0, of which waited for: 10 -> 0; matrix products, arithmetic and copies ran while one was open for 0% -> 0% of each run, Pallas kernels for 0% -> 0%
where the time goes in v1:
time: 121 us
  Pallas kernels  118 us (98%)
  local copies, waits for them, and re-layouts  2.44 us (2%)
    pallas_call x1, Pallas kernels, per_device(): pl.pallas_call(kernel, out_shape=(shape, shape), in_specs=[anywhere, anyw...  118 us
    unnamed x2, local copies, waits for them, and re-layouts  2.44 us

profile of v1, /device:TPU:1, one launch (start us, length us, event | category | flops | bytes accessed | tf_op | source)
XLA Modules:
  0.0 121.0 jit_solution(12414812363906041322)
XLA Ops:
  0.6 117.9 %relay.1 = (f32[2,4]{1,0:T(2,128)}, f32[2,4]{1,0:T(2,128)}) custom-call(bf16[64,256]{1,0:T(8,128)(2,1)} %bitcast.5, bf16[8192,256]{1,0:T(8,128)(2,1)} %bitcast.3, bf16[256,8192]{1,0:T(8,128)(2,1)} %bitcast.4, bf16[256,256]{1,0:T(8,128)(2,1)} %head_ref.1, f32[2,4]{1,0:T(2,128)} %reward_ref.1, s32[2,4]{1,0:T(2,128)} %action_ref.1), custom_call_target="tpu_custom_call" | custom-call | tf_op jit(solution)/shard_map/relay/pallas_call | solution.py:298
  118.6 1.2 %copy.10 = f32[2,4]{1,0:T(2,128)} copy(f32[2,4]{1,0:T(2,128)} %get-tuple-element.4) | data formatting | bytes 64
  119.8 1.2 %copy.11 = f32[2,4]{1,0:T(2,128)} copy(f32[2,4]{1,0:T(2,128)} %get-tuple-element.5) | data formatting | bytes 64

commit v2 on v1

v2 whole, which is shorter than its diff:
```python
import functools

import jax
import jax.numpy as jnp
from jax import lax
from jax.experimental import pallas as pl
from jax.experimental.pallas import tpu as pltpu
from jax.sharding import PartitionSpec as P

MESH = pl.DeviceIdType.MESH
SECTIONS = 8
PEERS = 32
ROWS = 64
WIDTH = 256
DEPTH = PEERS * WIDTH
CHUNKS = 8
AHEAD = (2, 1, 1)
PART = ROWS // CHUNKS
OWNED = 8
SCORE = 2 * WIDTH + 128
WHOLE = ()


FAR = (0, 1, 3, 2)


def place(tp):
    return tp // 16, lax.rem(tp // 4, 4), lax.rem(tp, 4)


def index(z, x, y):
    return z * 16 + x * 4 + y


def kernel(
    start_ref, target_ref, online_ref, head_ref, reward_ref, action_ref, value_ref, taken_ref,
    target, online, moved, hidden, shares, sends, result, product_head, both, scores, gathered, summed, finals, wide_finals,
    load_sem, move_sem, head_sem, row_sem, own_sem, all_sem, share_sem, move_out, all_out, next_out, share_out, score_sem, score_out, final_sem, final_out,
):
    section = lax.axis_index("section")
    me = lax.axis_index("tp")
    z, x, y = place(me)
    along_z = [z * 16, (1 - z) * 16]
    ring_x = [lax.rem(x + i, 4) * 4 for i in range(4)]
    ring_y = [lax.rem(y + i, 4) for i in range(4)]
    along_x = [ring_x[i] for i in FAR]
    along_y = [ring_y[i] for i in FAR]

    def peer(step):
        return along_z[step // 16] + along_x[step // 4 % 4] + along_y[step % 4]

    peers = range(PEERS - 1, 0, -1)
    odd = lax.rem(section, 2)
    even = odd == 0
    last = section == SECTIONS - 1
    spread = jnp.logical_and(even, section < SECTIONS - 2)
    whole = functools.reduce(jnp.logical_or, [section == s for s in WHOLE], False)
    split = jnp.logical_not(jnp.logical_or(whole, last))
    my_micro, bit = y // 2, lax.rem(y, 2)
    my_block = (1 - bit) * (1 - z) + bit * (2 + z)

    def owner(micro, block):
        return index(lax.rem((block + 1) // 2 + 1, 2), x, 2 * micro + block // 2)

    def remote(src, dst, out, sem, at_section, tp):
        return pltpu.make_async_remote_copy(
            src_ref=src, dst_ref=dst, send_sem=out, recv_sem=sem,
            device_id={"section": at_section, "tp": tp}, device_id_type=MESH,
        )

    def settle(ref, sem):
        pltpu.make_async_copy(ref, ref, sem).wait()

    def columns(tp):
        return pl.ds(pl.multiple_of(tp * WIDTH, WIDTH), WIDTH)

    load_online = pltpu.make_async_copy(online_ref, online, load_sem.at[0])
    load_online.start()

    @pl.when(jnp.logical_not(last))
    def _():
        pltpu.make_async_copy(target_ref, target, load_sem.at[1]).start()

    @pl.when(last)
    def _():
        pltpu.make_async_copy(target_ref.at[me], target.at[me], load_sem.at[1]).start()
        pltpu.make_async_copy(head_ref, moved.at[me], load_sem.at[2]).start()

    @pl.when(whole)
    def _():
        pltpu.make_async_copy(online_ref.at[:, columns(me)], moved.at[me], load_sem.at[2]).start()

    @pl.when(section == 0)
    def _():
        for c in range(CHUNKS):
            pltpu.make_async_copy(
                start_ref.at[pl.ds(c * PART, PART)], hidden.at[c, me], own_sem.at[c]
            ).start()

    barrier = pltpu.get_barrier_semaphore()

    def greet(at_section, tp):
        pl.semaphore_signal(
            barrier, inc=1, device_id={"section": at_section, "tp": tp}, device_id_type=MESH
        )

    for step in peers:
        greet(section, peer(step))

    @pl.when(jnp.logical_and(odd == 1, jnp.logical_not(last)))
    def _():
        for step in peers:
            greet(section - 1, peer(step))

    @pl.when(section > 0)
    def _():
        greet(section - 1, me)

    for micro in range(2):
        mine = owner(micro, section // 2)

        @pl.when(jnp.logical_not(jnp.logical_and(last, mine == me)))
        def _():
            greet(SECTIONS - 1, mine)

    @pl.when(spread)
    def _():
        pl.semaphore_wait(barrier, 2 * PEERS - 1)

    @pl.when(jnp.logical_not(jnp.logical_or(spread, last)))
    def _():
        pl.semaphore_wait(barrier, PEERS)

    @pl.when(jnp.logical_and(last, my_block != 3))
    def _():
        pl.semaphore_wait(barrier, PEERS - 1 + 16)

    @pl.when(jnp.logical_and(last, my_block == 3))
    def _():
        pl.semaphore_wait(barrier, PEERS - 1 + 15)

    most = PEERS - 1

    @pl.when(jnp.logical_not(last))
    def _():
        @pl.when(whole)
        def _():
            for step in peers:
                tp = peer(step)
                remote(online_ref.at[:, columns(tp)], moved.at[me], move_out, move_sem, section, tp).start()

        load_online.wait()
        settle(target, load_sem.at[1])

        @pl.when(whole)
        def _():
            settle(moved.at[0], load_sem.at[2])
            settle(moved.at[pl.ds(0, most)], move_sem)

            @pl.loop(0, PEERS)
            def _(tp):
                target[tp] = (
                    0.25 * moved[tp].astype(jnp.float32) + 0.75 * target[tp].astype(jnp.float32)
                ).astype(jnp.bfloat16)

    @pl.when(last)
    def _():
        seen = set()

        def near(dx, dy, dz):
            return along_z[dz] + ring_x[dx % 4] + ring_y[dy % 4]

        def arrived(dx, dy, dz):
            if (dx, dy, dz) not in seen:
                seen.add((dx, dy, dz))
                tp = near(dx, dy, dz)
                settle(moved.at[tp], head_sem.at[tp])

        def give_target(dx):
            for dz in (1, 0):
                for dy in (2, 1, 3, 0):
                    if (dx, dy, dz) != (0, 0, 0):
                        tp = near(dx, dy, dz)
                        remote(target_ref.at[tp], target.at[me], move_out, row_sem.at[me], section, tp).start()

        def pass_on(source, step):
            arrived(*source)
            tp = near(*source)
            remote(moved.at[tp], moved.at[tp], move_out, head_sem.at[tp], section, near(*step)).start()

        for dz in (1, 0):
            for dx in (1, 3, 0):
                for dy in (1, 3, 0):
                    if (dx, dy, dz) != (0, 0, 0):
                        remote(
                            head_ref, moved.at[me], move_out, head_sem.at[me], section, near(dx, dy, dz)
                        ).start()
        give_target(0)
        for dx in (1, 0, 3):
            for dz in (0, 1):
                pass_on((dx, 1, dz), (0, -1, 0))
        give_target(1)
        for dy in (0, 1, 3, 2):
            for dz in (0, 1):
                pass_on((1, dy, dz), (-1, 0, 0))
        give_target(3)
        give_target(2)
        load_online.wait()
        settle(target.at[0], load_sem.at[1])
        settle(moved.at[0], load_sem.at[2])
        product_head[...] = jnp.zeros_like(product_head)
        for dx in (0, 1, 3, 2):
            for dz in range(2):
                for dy in range(4):
                    if (dx, dy, dz) != (0, 0, 0):
                        arrived(dx, dy, dz)
                        tp = near(dx, dy, dz)
                        settle(target.at[tp], row_sem.at[tp])

            @pl.loop(0, 8)
            def _(i):
                tp = (i // 4) * 16 + ring_x[dx] + lax.rem(i, 4)
                blended = (
                    0.25 * online[:, columns(tp)].astype(jnp.float32) + 0.75 * target[tp].astype(jnp.float32)
                ).astype(jnp.bfloat16)
                product_head[...] += jnp.dot(blended, moved[tp], preferred_element_type=jnp.float32)

        both[:, :WIDTH] = moved[me]
        both[:, WIDTH:] = product_head[...].astype(jnp.bfloat16)

    def send(c):
        @pl.when(jnp.logical_or(even, split))
        def _():
            settle(hidden.at[c, 0], own_sem.at[c])

        @pl.when(even)
        def _():
            for step in peers:
                remote(
                    hidden.at[c, me], hidden.at[c, me], all_out.at[c], all_sem.at[c], section, peer(step)
                ).start()

        @pl.when(split)
        def _():
            own = hidden[c, me]
            for group in range(4):
                steps = [PEERS - 1 - 8 * group - u for u in range(8)]
                for step in steps:
                    tp = peer(step)
                    part = jnp.dot(
                        own, online[:, columns(tp)], preferred_element_type=jnp.float32
                    ).astype(jnp.bfloat16)
                    if step == 0:
                        shares[c, me] = part
                    else:
                        sends[c, tp] = part
                for step in steps:
                    if step > 0:
                        tp = peer(step)
                        remote(
                            sends.at[c, tp], shares.at[c, me], share_out.at[c], share_sem.at[c], section, tp
                        ).start()

    def reduce(c):
        @pl.when(jnp.logical_not(jnp.logical_or(even, split)))
        def _():
            settle(hidden.at[c, 0], own_sem.at[c])

        settle(hidden.at[c, pl.ds(0, most)], all_sem.at[c])
        product = jnp.zeros((PART, WIDTH), jnp.float32)
        square = jnp.zeros((PART, WIDTH), jnp.float32)
        for tp in range(PEERS):
            block = hidden[c, tp]
            product += jnp.dot(block, target[tp], preferred_element_type=jnp.float32)
            wide = block.astype(jnp.float32)
            square += wide * wide
        scale = lax.rsqrt(jnp.sum(square, axis=1, keepdims=True) * (1.0 / DEPTH) + 1e-06)
        own = hidden[c, me].astype(jnp.float32)

        @pl.when(split)
        def _():
            settle(shares.at[c, pl.ds(0, most)], share_sem.at[c])
            total = jnp.zeros((PART, WIDTH), jnp.float32)
            for tp in range(PEERS):
                total += shares[c, tp].astype(jnp.float32)
            result[c] = (own + scale * (0.75 * product + 0.25 * total)).astype(jnp.bfloat16)

        @pl.when(whole)
        def _():
            result[c] = (own + scale * product).astype(jnp.bfloat16)

        @pl.when(spread)
        def _():
            for step in peers:
                remote(
                    result.at[c], hidden.at[c, me], next_out.at[c], all_sem.at[c], section + 1, peer(step)
                ).start()

        remote(result.at[c], hidden.at[c, me], next_out.at[c], own_sem.at[c], section + 1, me).start()

    @pl.when(jnp.logical_not(last))
    def _():
        ahead = jnp.where(section == 0, AHEAD[0], jnp.where(even, AHEAD[2], AHEAD[1]))

        @pl.loop(0, CHUNKS + max(AHEAD))
        def _(step):
            @pl.when(step < CHUNKS)
            def _():
                send(step)

            @pl.when(jnp.logical_and(step >= ahead, step < CHUNKS + ahead))
            def _():
                reduce(step - ahead)

    @pl.when(last)
    def _():
        @pl.loop(0, CHUNKS)
        def _(c):
            settle(hidden.at[c, 0], own_sem.at[c])
            own = hidden[c, me]
            wide = own.astype(jnp.float32)
            scores[c, :, : 2 * WIDTH] = jnp.dot(own, both[...], preferred_element_type=jnp.float32)
            scores[c, :, 2 * WIDTH :] = jnp.broadcast_to(
                jnp.sum(wide * wide, axis=1, keepdims=True), (OWNED, 128)
            )
            first = owner(c // 4, lax.rem(c, 4))
            for column in range(4):
                tp = first + (column - x) * 4

                @pl.when(tp == me)
                def _():
                    gathered[me] = scores[c]

                @pl.when(tp != me)
                def _():
                    remote(scores.at[c], gathered.at[me], score_out, score_sem, section, tp).start()

        settle(gathered.at[pl.ds(0, most)], score_sem)
        total = jnp.zeros((OWNED, SCORE), jnp.float32)
        for tp in range(PEERS):
            total += gathered[tp]
        scale = lax.rsqrt(total[:, 2 * WIDTH : 2 * WIDTH + 1] * (1.0 / DEPTH) + 1e-06)
        summed[...] = total[:, :WIDTH] + scale * total[:, WIDTH : 2 * WIDTH]
        for i in range(16):
            at_section = 2 * my_block + i // 8
            tp = index((i // 4) % 2, x, i % 4)
            local = jnp.logical_and(at_section == section, tp == me)

            @pl.when(local)
            def _():
                pltpu.make_async_copy(summed, finals.at[my_micro], final_sem.at[my_micro]).start()

            @pl.when(jnp.logical_not(local))
            def _():
                remote(
                    summed, finals.at[my_micro], final_out, final_sem.at[my_micro], at_section, tp
                ).start()

    @pl.loop(0, CHUNKS)
    def _(c):
        @pl.when(split)
        def _():
            settle(sends.at[c, pl.ds(0, most)], share_out.at[c])

        @pl.when(even)
        def _():
            settle(hidden.at[c, pl.ds(0, most)], all_out.at[c])

        @pl.when(spread)
        def _():
            settle(hidden.at[c], next_out.at[c])

        @pl.when(jnp.logical_not(jnp.logical_or(spread, last)))
        def _():
            settle(hidden.at[c, 0], next_out.at[c])

    @pl.when(whole)
    def _():
        settle(moved.at[pl.ds(0, most)], move_out)

    @pl.when(last)
    def _():
        settle(moved.at[pl.ds(0, most)], move_out)
        settle(target.at[pl.ds(0, most)], move_out)

    lane = lax.broadcasted_iota(jnp.int32, (OWNED, WIDTH), 1)
    row = lax.broadcasted_iota(jnp.int32, (OWNED, WIDTH), 0) - 4 * odd
    for micro in range(2):
        settle(finals.at[micro], final_sem.at[micro])
        q = finals[micro]
        action = jnp.zeros((OWNED, WIDTH), jnp.int32)
        for token in range(4):
            action = jnp.where(row == token, action_ref[micro, token], action)
        best = jnp.max(q, axis=1, keepdims=True)
        taken = jnp.sum(jnp.where(lane == action, q, 0.0), axis=1, keepdims=True)
        best = jnp.sum(jnp.where(lane == row, best, 0.0), axis=0, keepdims=True)
        taken = jnp.sum(jnp.where(lane == row, taken, 0.0), axis=0, keepdims=True)
        value_ref[pl.ds(micro, 1), :] = reward_ref[pl.ds(micro, 1), :] + 0.98 * best[:, :4]
        taken_ref[pl.ds(micro, 1), :] = taken[:, :4]

    @pl.when(last)
    def _():
        settle(gathered.at[pl.ds(0, most)], score_out)

        @pl.when(my_block != 3)
        def _():
            settle(wide_finals.at[pl.ds(0, 16)], final_out)

        @pl.when(my_block == 3)
        def _():
            settle(wide_finals.at[pl.ds(0, 15)], final_out)


def per_device(start_tokens, target_weight, online_weight, head_weight, reward, action_bin):
    bf16, f32 = jnp.bfloat16, jnp.float32
    dma = pltpu.SemaphoreType.DMA
    shape = jax.ShapeDtypeStruct(reward.shape, f32)
    anywhere = pl.BlockSpec(memory_space=pl.ANY)
    vmem = pl.BlockSpec(memory_space=pltpu.VMEM)
    blocks = pltpu.VMEM((CHUNKS, PEERS, PART, WIDTH), bf16)
    weight = pltpu.VMEM((PEERS, WIDTH, WIDTH), bf16)
    return pl.pallas_call(
        kernel,
        out_shape=(shape, shape),
        in_specs=[anywhere, anywhere, anywhere, anywhere, vmem, pl.BlockSpec(memory_space=pltpu.SMEM)],
        out_specs=(vmem, vmem),
        scratch_shapes=[
            weight,
            pltpu.VMEM((WIDTH, DEPTH), bf16),
            weight,
            blocks,
            blocks,
            blocks,
            pltpu.VMEM((CHUNKS, PART, WIDTH), bf16),
            pltpu.VMEM((WIDTH, WIDTH), f32),
            pltpu.VMEM((WIDTH, 2 * WIDTH), bf16),
            pltpu.VMEM((CHUNKS, OWNED, SCORE), f32),
            pltpu.VMEM((PEERS, OWNED, SCORE), f32),
            pltpu.VMEM((OWNED, WIDTH), f32),
            pltpu.VMEM((2, OWNED, WIDTH), f32),
            pltpu.VMEM((16, OWNED, WIDTH), f32),
            dma((3,)),
            dma,
            dma((PEERS,)),
            dma((PEERS,)),
            dma((CHUNKS,)),
            dma((CHUNKS,)),
            dma((CHUNKS,)),
            dma,
            dma((CHUNKS,)),
            dma((CHUNKS,)),
            dma((CHUNKS,)),
            dma,
            dma,
            dma((2,)),
            dma,
        ],
        name="relay",
        compiler_params=pltpu.CompilerParams(collective_id=0, has_side_effects=True),
    )(
        start_tokens.reshape(ROWS, WIDTH),
        target_weight.reshape(PEERS, WIDTH, WIDTH),
        online_weight.reshape(WIDTH, DEPTH),
        head_weight,
        reward,
        action_bin,
    )


def solution(mesh):
    in_specs = (
        P(None, None, "tp"),
        P("section", None, "tp"),
        P("section", "tp", None),
        P("tp", None),
        P(None, "section"),
        P(None, "section"),
    )
    out_specs = (P(None, "section"), P(None, "section"))
    return jax.shard_map(
        per_device, mesh=mesh, in_specs=in_specs, out_specs=out_specs, check_vma=False
    )
```

time: 121 us -> 99.6 us (0.82)
  Pallas kernels: 118 us -> 96.1 us
    pallas_call x1, Pallas kernels: 118 us -> 96.1 us  [per_device(): pl.pallas_call(kernel, out_shape=(shape, shape), in_specs=[anywhere, anyw...]
where the time goes in v2:
time: 99.6 us; the launch traced here: 99.2 us
  Pallas kernels  96.1 us (96%)
  local copies, waits for them, and re-layouts  2.44 us (2%)
    pallas_call x1, Pallas kernels, per_device(): pl.pallas_call(kernel, out_shape=(shape, shape), in_specs=[anywhere, anyw...  96.1 us
    unnamed x2, local copies, waits for them, and re-layouts  2.44 us

profile of v2, /device:TPU:1, one launch (start us, length us, event | category | flops | bytes accessed | tf_op | source)
XLA Modules:
  0.0 99.2 jit_solution(15671461257522676512)
XLA Ops:
  0.6 96.1 %relay.1 = (f32[2,4]{1,0:T(2,128)}, f32[2,4]{1,0:T(2,128)}) custom-call(bf16[64,256]{1,0:T(8,128)(2,1)} %bitcast.5, bf16[32,256,256]{2,1,0:T(8,128)(2,1)} %bitcast.3, bf16[256,8192]{1,0:T(8,128)(2,1)} %bitcast.4, bf16[256,256]{1,0:T(8,128)(2,1)} %head_ref.1, f32[2,4]{1,0:T(2,128)} %reward_ref.1, s32[2,4]{1,0:T(2,128)} %action_ref.1), custom_call_target="tpu_custom_call" | custom-call | tf_op jit(solution)/shard_map/relay/pallas_call | solution.py:422
  96.7 1.2 %copy.10 = f32[2,4]{1,0:T(2,128)} copy(f32[2,4]{1,0:T(2,128)} %get-tuple-element.4) | data formatting | bytes 64
  97.9 1.2 %copy.11 = f32[2,4]{1,0:T(2,128)} copy(f32[2,4]{1,0:T(2,128)} %get-tuple-element.5) | data formatting | bytes 64
